TPU v7x, 256 devices: a whole 4x4x8 slice. The times are simulated.
256 devices in a mesh: ctx: 32 (over z, y_hi, core), fsdp: 8 (over x, y_lo).
Axes of the slice: x: 4, y: 4 (y_hi: 2, y_lo: 2; y = y_hi * 2 + y_lo), z: 8, core: 2. Of those that a mesh axis runs over, the one named last changes fastest.
Arguments:
- xbc_raw: bfloat16 [8, 4096, 2560], P('fsdp', 'ctx'), may hold values from -6 to 6
- dt_raw: float32 [8, 4096, 64], P('fsdp', 'ctx'), as said below
- a_log: float32 [64], replicated, may hold values from 0 to 2.7726, as said below
- skip: float32 [64], replicated, may hold values from 0.5 to 1.5
- conv_weight: bfloat16 [4, 2560], P(None, 'fsdp'), may hold values from -3 to 3
- conv_bias: bfloat16 [2560], P('fsdp'), may hold values from -3 to 3
- grad_y: bfloat16 [8, 4096, 2048], P('fsdp', 'ctx'), may hold values from -6 to 6
Outputs:
- grad_xbc_raw: bfloat16 [8, 4096, 2560], P('fsdp', 'ctx')
- grad_dt_raw: float32 [8, 4096, 64], P('fsdp', 'ctx')
- grad_a_log: float32 [64], replicated
- grad_skip: float32 [64], replicated
- grad_conv_weight: float32 [4, 2560], P(None, 'fsdp')
- grad_conv_bias: float32 [2560], P('fsdp')
Inputs may be any that keep to these rules, and one draw needn't show every extreme that they name: Each head's decay coefficient exp(a_log) lies between 1 and 16. softplus(dt_raw) is a positive step size.
All inputs are finite; a program needn't handle non-finite values.
Results may differ from a plain program's by a relative error of at most 0.0007.
Values may be sent and summed in bfloat16 or wider, within the bound.
A program may use at most 256 MiB of HBM per device.

v0:
```python
import math

import jax
import jax.numpy as jnp
from jax import lax
from jax.sharding import PartitionSpec as P

HW = 64
GW = 4
P_SIZE = 32
N = 64
KW = 4
SPAN = 128


HIGHEST_PREC = lax.Precision.HIGHEST


def from_behind(value, axis, by):
    length = lax.axis_size(axis)
    pairs = [(i, i + by) for i in range(length) if 0 <= i + by < length]
    return lax.ppermute(value, axis, pairs)


def carried_in(value, axis, join, neutral, backward):
    count, mine = (lax.axis_size(axis), lax.axis_index(axis))
    pieces = jax.tree.map(lambda part: lax.all_gather(part, axis), value)
    if backward:
        pieces = jax.tree.map(lambda part: part[::-1], pieces)
        mine = count - 1 - mine
    running = jax.tree.map(
        lambda part, zero: jnp.full_like(part, 0) + jnp.asarray(zero, part.dtype), value, neutral
    )

    def lap(position, running):
        longer = join(running, jax.tree.map(lambda part: part[position], pieces))
        return jax.tree.map(lambda new, old: jnp.where(position < mine, new, old), longer, running)

    return lax.fori_loop(0, count - 1, lap, running)


def compose(earlier, later):
    return (earlier[0] * later[0], later[0][..., None, None] * earlier[1] + later[1])


def body(xbc_raw, dt_raw, a_log, skip, conv_weight, conv_bias, grad_y):
    raw_rows = xbc_raw[0]
    tok_rows = raw_rows.shape[0]
    per_group = HW // GW
    inner_width = HW * P_SIZE
    blocks = tok_rows // SPAN
    weight_all, bias_all = (
        lax.all_gather(conv_weight, "fsdp", axis=1, tiled=True),
        lax.all_gather(conv_bias, "fsdp", axis=0, tiled=True),
    )
    weight_f = weight_all.astype(jnp.float32)
    bias_f = bias_all.astype(jnp.float32)
    tail_rows = raw_rows[tok_rows - (KW - 1) :]
    rows_prev = from_behind(tail_rows, "ctx", 1)
    padded = jnp.concatenate([rows_prev, raw_rows], 0).astype(jnp.float32)
    pre_act = bias_f + sum(
        (weight_f[tap_idx] * padded[tap_idx : tap_idx + tok_rows] for tap_idx in range(KW))
    )
    gate_vals = jax.nn.sigmoid(pre_act)
    conv_out = pre_act * gate_vals
    x_all = conv_out[:, :inner_width].reshape(blocks, SPAN, GW, per_group, P_SIZE)
    b_all = conv_out[:, inner_width : inner_width + GW * N].reshape(blocks, SPAN, GW, N)
    c_all = conv_out[:, inner_width + GW * N :].reshape(blocks, SPAN, GW, N)
    steps_raw = dt_raw[0]
    step_size = jax.nn.softplus(steps_raw)
    rate_head = jnp.exp(a_log)
    log_decay = -rate_head * step_size
    dt_c = step_size.reshape(blocks, SPAN, GW, per_group)
    la_c = log_decay.reshape(blocks, SPAN, GW, per_group)
    d_out = grad_y[0].astype(jnp.float32).reshape(blocks, SPAN, GW, per_group, P_SIZE)
    cum_log = jnp.cumsum(la_c, 1)
    exp_cum = jnp.exp(cum_log)
    last_log = cum_log[:, -1]
    span_decay = jnp.exp(last_log)
    tail_decay = jnp.exp(last_log[:, None] - cum_log)
    inputs = dt_c[..., None] * x_all
    local_end = jnp.einsum(
        "csgkp,csgn->cgkpn", tail_decay[..., None] * inputs, b_all, precision=HIGHEST_PREC
    )
    local_adj = jnp.einsum(
        "ctgkp,ctgn->cgkpn", exp_cum[..., None] * d_out, c_all, precision=HIGHEST_PREC
    )
    unit_decay = jnp.ones((GW, per_group), jnp.float32)
    zero_state = jnp.zeros((GW, per_group, P_SIZE, N), jnp.float32)
    dev_decay = unit_decay
    fwd_total = zero_state
    span_idx = 0
    fwd_total = span_decay[span_idx][..., None, None] * fwd_total + local_end[span_idx]
    dev_decay = dev_decay * span_decay[span_idx]
    back_total = zero_state
    for span_idx in reversed(range(blocks)):
        back_total = local_adj[span_idx] + span_decay[span_idx][..., None, None] * back_total
    state_in = carried_in((dev_decay, fwd_total), "ctx", compose, (unit_decay, zero_state), False)[
        1
    ]
    adjoint_end = carried_in(
        (dev_decay, back_total), "ctx", compose, (unit_decay, zero_state), True
    )[1]
    cum_t = jnp.transpose(cum_log, (0, 2, 3, 1))
    lower_mask = jnp.tril(jnp.ones((SPAN, SPAN), bool))
    log_gap = cum_t[..., :, None] - cum_t[..., None, :]
    mixing = jnp.where(lower_mask, jnp.exp(jnp.where(lower_mask, log_gap, 0.0)), 0.0)
    scores = jnp.einsum("ctgn,csgn->cgts", c_all, b_all, precision=HIGHEST_PREC)
    weights = scores[:, :, None] * mixing
    d_weights = jnp.einsum("ctgkp,csgkp->cgkts", d_out, inputs, precision=HIGHEST_PREC)
    d_inputs = jnp.einsum("cgkts,ctgkp->csgkp", weights, d_out, precision=HIGHEST_PREC)
    flow_terms = d_weights * weights
    d_scores = jnp.sum(d_weights * mixing, 2)
    d_cum = jnp.transpose(jnp.sum(flow_terms, -1) - jnp.sum(flow_terms, -2), (0, 3, 1, 2))
    d_c = jnp.einsum("cgts,csgn->ctgn", d_scores, b_all, precision=HIGHEST_PREC)
    d_b = jnp.einsum("cgts,ctgn->csgn", d_scores, c_all, precision=HIGHEST_PREC)
    carried = state_in
    span_idx = 0
    start_list = [carried]
    end_list = []
    carried = adjoint_end
    for span_idx in reversed(range(blocks)):
        end_list.append(carried)
        carried = local_adj[span_idx] + span_decay[span_idx][..., None, None] * carried
    start_state = jnp.stack(start_list)
    end_adjoint = jnp.stack(end_list[::-1])
    from_state = jnp.einsum("ctgn,cgkpn->ctgkp", c_all, start_state, precision=HIGHEST_PREC)
    d_cum = d_cum + exp_cum * jnp.sum(d_out * from_state, -1)
    d_c = d_c + jnp.einsum(
        "ctgkp,cgkpn->ctgn", exp_cum[..., None] * d_out, start_state, precision=HIGHEST_PREC
    )
    pulled = jnp.einsum("cgkpn,csgn->csgkp", end_adjoint, b_all, precision=HIGHEST_PREC)
    d_inputs = d_inputs + tail_decay[..., None] * pulled
    d_b = d_b + jnp.einsum(
        "csgkp,cgkpn->csgn", tail_decay[..., None] * inputs, end_adjoint, precision=HIGHEST_PREC
    )
    d_tail = tail_decay * jnp.sum(inputs * pulled, -1)
    d_last = jnp.sum(d_tail, 1) + span_decay * jnp.sum(end_adjoint * start_state, (-2, -1))
    d_cum = d_cum - d_tail
    d_cum = d_cum.at[:, -1].add(d_last)
    d_log = jnp.flip(jnp.cumsum(jnp.flip(d_cum, 1), 1), 1)
    d_step = jnp.sum(d_inputs * x_all, -1) - rate_head.reshape(GW, per_group) * d_log
    d_x = d_inputs * dt_c[..., None] + skip.reshape(GW, per_group)[..., None] * d_out
    d_skip_local = jnp.sum(d_out * x_all, (0, 1, 4)).reshape(HW)
    d_alog_local = jnp.sum(d_log * la_c, (0, 1)).reshape(HW)
    d_dt_raw = d_step.reshape(tok_rows, HW) * jax.nn.sigmoid(steps_raw)
    d_conv = jnp.concatenate(
        [
            d_x.reshape(tok_rows, inner_width),
            d_b.reshape(tok_rows, GW * N),
            d_c.reshape(tok_rows, GW * N),
        ],
        1,
    )
    d_pre = d_conv * gate_vals * (1.0 + pre_act * (1.0 - gate_vals))
    rows_next = from_behind(d_pre[: KW - 1], "ctx", -1)
    extended = jnp.concatenate([d_pre, rows_next], 0)
    d_raw = sum(
        (
            weight_f[tap_idx] * extended[KW - 1 - tap_idx : KW - 1 - tap_idx + tok_rows]
            for tap_idx in range(KW)
        )
    )
    d_weight = jnp.stack(
        [jnp.sum(d_pre * padded[tap_idx : tap_idx + tok_rows], 0) for tap_idx in range(KW)]
    )
    d_bias = jnp.sum(d_pre, 0)
    grad_scale = 1.0 / math.sqrt(tok_rows * lax.axis_size("ctx") * lax.axis_size("fsdp"))
    summed = lax.psum((d_weight, d_bias), "ctx")
    total_weight, total_bias = (
        lax.psum_scatter(summed[0], "fsdp", scatter_dimension=1, tiled=True),
        lax.psum_scatter(summed[1], "fsdp", scatter_dimension=0, tiled=True),
    )
    head_alog, head_skip = lax.psum((d_alog_local, d_skip_local), ("ctx", "fsdp"))
    return (
        d_raw.astype(jnp.bfloat16)[None],
        d_dt_raw[None],
        head_alog * grad_scale,
        head_skip * grad_scale,
        total_weight * grad_scale,
        total_bias * grad_scale,
    )


def solution(mesh):
    in_specs = (
        P("fsdp", "ctx", None),
        P("fsdp", "ctx", None),
        P(),
        P(),
        P(None, "fsdp"),
        P("fsdp"),
        P("fsdp", "ctx", None),
    )
    out_specs = (
        P("fsdp", "ctx", None),
        P("fsdp", "ctx", None),
        P(),
        P(),
        P(None, "fsdp"),
        P("fsdp"),
    )
    return jax.shard_map(body, mesh=mesh, in_specs=in_specs, out_specs=out_specs, check_vma=False)
```

profile of v0, /device:TPU:1, one launch (start us, length us, event | category | flops | bytes accessed | tf_op | source)
XLA Modules:
  0.0 813.6 jit_solution(4694572560234044566)
XLA Ops:
  8.1 6.2 collective-permute-start
  14.3 22.0 %all-gather.3 = bf16[8,320,4]{1,2,0:T(4,128)(2,1)S(1)} all-gather(bf16[1,320,4]{1,2,0:T(4,128)(2,1)} %bitcast.187), channel_id=1, replica_groups=mesh['ctx'=32,'fsdp'=8] {'fsdp'}, dimensions={0}, use_global_device_ids=true | all-gather | bytes 23040 | tf_op jit(solution)/shard_map/all_gather | solution.py:53
  42.4 15.4 %all-reduce = bf16[2560]{0:T(1024)(128)(2,1)S(1)} all-reduce(bf16[2560]{0:T(1024)(128)(2,1)S(1)} %dynamic-update-slice.3), channel_id=1, replica_groups=mesh['ctx'=32,'fsdp'=8] {'fsdp'}, use_global_device_ids=true, to_apply=%add | all-reduce | flops 2560 | bytes 10240
  59.2 4.1 fusion.30
  63.3 2.0 convolution_add_fusion.1
  66.5 2.1 convolution_add_fusion
  68.7 53.2 %all-gather = f32[32,1,4,16]{3,2,1,0:T(4,128)S(1)} all-gather(f32[1,1,4,16]{3,2,1,0:T(4,128)S(1)} %copy.145), channel_id=2, replica_groups=mesh['ctx'=32,'fsdp'=8] {'ctx'}, dimensions={0}, use_global_device_ids=true | all-gather | bytes 8448 | tf_op jit(solution)/shard_map/all_gather | solution.py:27
  122.5 1.7 copy.139
  130.8 7.5 fusion.6
  138.3 162.6 %all-gather.7.cloned.1.call-done = f32[128,16,32,64]{3,2,1,0:T(8,128)} async-done(((f32[4,16,32,64]{3,2,1,0:T(8,128)}), f32[128,16,32,64]{3,2,1,0:T(8,128)}) %all-gather.7.cloned.1.call-update) | async-done | bytes 16777232 | tf_op jit(solution)/shard_map/all_gather | solution.py:27
  300.9 23.8 %rev.14 = f32[32,4,16,32,64]{4,3,2,1,0:T(8,128)} reverse(f32[32,4,16,32,64]{4,3,2,1,0:T(8,128)} %bitcast.153), dimensions={0} | reverse | bytes 33554432 | tf_op jit(solution)/shard_map/rev | solution.py:29
  324.7 67.5 %while.29 = (s32[]{:T(128)}, f32[4,16,32,64]{3,2,1,0:T(8,128)S(1)}, s32[]{:T(128)}, f32[32,4,16]{2,1,0:T(4,128)}, f32[32,4,16,32,64]{4,3,2,1,0:T(8,128)}, /*index=5*/s32[]{:T(128)}, s32[]{:T(128)}) while((s32[]{:T(128)}, f32[4,16,32,64]{3,2,1,0:T(8,128)S(1)}, s32[]{:T(128)}, f32[32,4,16]{2,1,0:T(4,128)}, ...), condition=%wide.region_2.3_spmd.clone, body=%wide.region_1.2_spmd.clone.sunk | while | flops 524292 | bytes 1573737 | solution.py:39
  325.3 1.5 fusion.78
  327.5 1.5 fusion.78
  329.7 1.5 fusion.78
  331.8 1.5 fusion.78
  333.9 1.5 fusion.78
  336.1 1.5 fusion.78
  338.3 1.5 fusion.78
  340.5 1.5 fusion.78
  342.6 1.5 fusion.78
  344.8 1.5 fusion.78
  347.0 1.5 fusion.78
  349.1 1.5 fusion.78
  351.2 1.5 fusion.78
  353.4 1.5 fusion.78
  355.6 1.5 fusion.78
  357.8 1.5 fusion.78
  359.9 1.5 fusion.78
  362.1 1.5 fusion.78
  370.7 1.8 fusion.78
  373.2 1.6 fusion.78
  377.6 1.5 fusion.78
  392.2 1.9 convolution_bitcast_fusion.1
  394.1 1.9 convolution_bitcast_fusion.3
  396.0 131.6 %all-gather.9.cloned.1.call-done = f32[128,16,32,64]{3,2,1,0:T(8,128)} async-done(((f32[4,16,32,64]{3,2,1,0:T(8,128)}), f32[128,16,32,64]{3,2,1,0:T(8,128)}) %all-gather.9.cloned.1.call-update) | async-done | bytes 16777232 | tf_op jit(solution)/shard_map/all_gather | solution.py:27
  527.6 66.9 %while.30 = (s32[]{:T(128)}, f32[4,16,32,64]{3,2,1,0:T(8,128)S(1)}, s32[]{:T(128)}, f32[32,4,16]{2,1,0:T(4,128)}, f32[32,4,16,32,64]{4,3,2,1,0:T(8,128)}, /*index=5*/s32[]{:T(128)}, s32[]{:T(128)}) while((s32[]{:T(128)}, f32[4,16,32,64]{3,2,1,0:T(8,128)S(1)}, s32[]{:T(128)}, f32[32,4,16]{2,1,0:T(4,128)}, ...), condition=%wide.region_5.6_spmd.clone, body=%wide.region_4.5_spmd.clone.sunk | while | flops 524292 | bytes 1573737 | solution.py:39
  594.5 2.9 convolution_bitcast_fusion.2
  599.5 6.0 multiply_reduce_fusion.5
  605.5 3.6 multiply_reduce_fusion.3
  609.8 2.4 copy.166
  612.3 1.7 fusion.31
  617.9 76.8 %all-reduce.2 = (f32[64]{0:T(128)S(1)}, f32[64]{0:T(128)S(1)}) all-reduce(f32[64]{0:T(128)S(1)} %reshape.418, f32[64]{0:T(128)S(1)} %copy-done.48), channel_id=1, replica_groups=mesh['ctx'=32,'fsdp'=8] {'ctx','fsdp'}, use_global_device_ids=true, to_apply=%region_15.16 | all-reduce | flops 128 | bytes 1024 | tf_op jit(solution)/shard_map/psum | solution.py:174
  696.2 2.9 collective-permute-start.1
  699.6 24.9 %all-reduce.1 = f32[2560]{0:T(1024)S(1)} all-reduce(f32[2560]{0:T(1024)S(1)} %copy-done.36), channel_id=6, replica_groups=mesh['ctx'=32,'fsdp'=8] {'fsdp'}, use_global_device_ids=true, to_apply=%region_27.28.clone | all-reduce | flops 2560 | bytes 20480
  724.7 1.5 copy.150
  726.2 5.9 fusion.39
  734.2 71.7 %all-reduce.3 = (f32[4,320]{1,0:T(4,128)S(1)}, f32[320]{0:T(512)S(1)}) all-reduce(f32[4,320]{1,0:T(4,128)S(1)} %copy.167, f32[320]{0:T(512)S(1)} %dynamic-slice.10), channel_id=1, replica_groups=mesh['ctx'=32,'fsdp'=8] {'ctx'}, use_global_device_ids=true, to_apply=%region_23.24 | all-reduce | flops 1600 | bytes 12800 | tf_op jit(solution)/shard_map/psum | solution.py:169
  (274 shorter events, 128.5 us)
Async XLA Ops:
  7.2 33.4 %copy-start.12 = (bf16[1,128,2560]{2,1,0:T(8,128)(2,1)S(1)}, bf16[1,128,2560]{2,1,0:T(8,128)(2,1)}, u32[]{:S(2)}) copy-start(bf16[1,128,2560]{2,1,0:T(8,128)(2,1)} %param.13) | copy-start | bytes 1966084
  7.2 32.5 %copy-start.18 = (f32[1,128,64]{1,2,0:T(8,128)S(1)}, f32[1,128,64]{1,2,0:T(8,128)}, u32[]{:S(2)}) copy-start(f32[1,128,64]{1,2,0:T(8,128)} %param.14) | copy-start | bytes 98308
  7.2 293.7 %all-gather.7.cloned.1.call-start = ((), (), s32[]{:S(2)}) async-start(), calls=%async_computation.1 | async-start | bytes 34603008 | tf_op jit(solution)/shard_map/all_gather | solution.py:27
  8.1 50.1 %collective-permute-start = (bf16[3,2560]{1,0:T(4,128)(2,1)S(1)}, bf16[3,2560]{1,0:T(4,128)(2,1)S(1)}, u32[]{:S(2)}, u32[]{:S(2)}) collective-permute-start(bf16[3,2560]{1,0:T(4,128)(2,1)S(1)} %slice_bitcast_fusion), channel_id=1, source_target_pairs={{0,8},{8,16},{16,24},{24,32},{32,40},{40,48},{48,56},{56,64},{64,7... | collective-permute-start | bytes 46088 | tf_op jit(solution)/shard_map/ppermute | solution.py:22
  38.7 2.2 copy-start.46
  38.7 3.5 copy-start.47
  38.7 19.2 %copy-start.17 = (bf16[1,128,2048]{2,1,0:T(8,128)(2,1)S(1)}, bf16[1,128,2048]{2,1,0:T(8,128)(2,1)}, u32[]{:S(2)}) copy-start(bf16[1,128,2048]{2,1,0:T(8,128)(2,1)} %param.19) | copy-start | bytes 1572868
  38.9 19.0 %copy-start.7 = (f32[1,128,4,16]{3,2,1,0:T(4,128)}, f32[1,128,4,16]{3,2,1,0:T(4,128)S(1)}, u32[]{:S(2)}) copy-start(f32[1,128,4,16]{3,2,1,0:T(4,128)S(1)} %fusion.55) | copy-start | bytes 98308
  39.0 18.9 %copy-start.11 = (f32[1,128,4,16]{1,3,2,0:T(8,128)}, f32[1,128,4,16]{1,3,2,0:T(8,128)S(1)}, u32[]{:S(2)}) copy-start(f32[1,128,4,16]{1,3,2,0:T(8,128)S(1)} %copy.143) | copy-start | bytes 98308
  39.7 18.2 %copy-start.38 = (f32[4,16]{1,0:T(4,128)}, f32[4,16]{1,0:T(4,128)S(1)}, u32[]{:S(2)}) copy-start(f32[4,16]{1,0:T(4,128)S(1)} %get-tuple-element.327) | copy-start | bytes 772
  40.5 18.6 %copy-start.30 = (f32[2560]{0:T(1024)}, f32[2560]{0:T(1024)S(1)}, u32[]{:S(2)}) copy-start(f32[2560]{0:T(1024)S(1)} %get-tuple-element.285) | copy-start | bytes 30724
  40.5 18.6 %copy-start.32 = (f32[2560]{0:T(1024)}, f32[2560]{0:T(1024)S(1)}, u32[]{:S(2)}) copy-start(f32[2560]{0:T(1024)S(1)} %get-tuple-element.286) | copy-start | bytes 30724
  40.5 18.6 %copy-start.34 = (f32[2560]{0:T(1024)}, f32[2560]{0:T(1024)S(1)}, u32[]{:S(2)}) copy-start(f32[2560]{0:T(1024)S(1)} %get-tuple-element.287) | copy-start | bytes 30724
  58.2 7.3 copy-start.2
  59.1 4.2 copy-start
  59.2 4.2 copy-start.25
  63.3 3.1 copy-start.5
  65.4 462.2 %all-gather.9.cloned.1.call-start = ((), (), s32[]{:S(2)}) async-start(), calls=%async_computation.2 | async-start | bytes 34603008 | tf_op jit(solution)/shard_map/all_gather | solution.py:27
  66.4 2.2 copy-start.29
  68.5 61.0 %copy-start.6 = (f32[128,256]{0,1:T(8,128)S(1)}, f32[128,256]{0,1:T(8,128)}, u32[]{:S(2)}) copy-start(f32[128,256]{0,1:T(8,128)} %copy-done.5) | copy-start | bytes 393220
  68.5 62.3 %copy-start.22 = (f32[128,4,16]{0,2,1:T(8,128)S(1)}, f32[128,4,16]{0,2,1:T(8,128)}, u32[]{:S(2)}) copy-start(f32[128,4,16]{0,2,1:T(8,128)} %get-tuple-element.333) | copy-start | bytes 98308
  68.5 664.6 %reduce-scatter.4.cloned.1.call-start = ((), (), s32[]{:S(2)}) async-start(), calls=%async_computation.3 | async-start | bytes 1474560
  121.9 16.4 %copy-start.20 = (f32[32,1,4,16]{3,2,1,0:T(4,128)}, f32[32,1,4,16]{3,2,1,0:T(4,128)S(1)}, u32[]{:S(2)}) copy-start(f32[32,1,4,16]{3,2,1,0:T(4,128)S(1)} %all-gather) | copy-start | bytes 24580
  392.1 2.0 copy-start.14
  392.1 2.0 copy-start.23
  597.5 1.9 copy-start.3
  597.5 1.9 copy-start.8
  597.5 1.9 copy-start.15
  597.5 1.9 copy-start.24
  597.5 1.9 copy-start.27
  597.5 1.9 copy-start.37
  597.6 1.9 copy-start.43
  597.6 1.9 copy-start.45
  599.5 6.0 copy-start.1
  599.5 6.0 copy-start.4
  609.8 2.4 copy-start.9
  612.2 1.7 copy-start.16
  612.2 2.7 copy-start.39
  613.9 3.7 copy-start.19
  613.9 3.7 copy-start.40
  613.9 3.7 copy-start.42
  613.9 3.7 copy-start.44
  614.0 3.9 copy-start.48
  617.3 82.3 %copy-start.36 = (f32[2560]{0:T(1024)S(1)}, f32[2560]{0:T(1024)}, u32[]{:S(2)}) copy-start(f32[2560]{0:T(1024)} %get-tuple-element.281) | copy-start | bytes 30724
  695.8 30.4 %copy-start.31 = (f32[2560]{0:T(1024)S(1)}, f32[2560]{0:T(1024)}, u32[]{:S(2)}) copy-start(f32[2560]{0:T(1024)} %copy-done.30) | copy-start | bytes 30724
  695.8 30.4 %copy-start.33 = (f32[2560]{0:T(1024)S(1)}, f32[2560]{0:T(1024)}, u32[]{:S(2)}) copy-start(f32[2560]{0:T(1024)} %copy-done.32) | copy-start | bytes 30724
  695.8 30.4 %copy-start.35 = (f32[2560]{0:T(1024)S(1)}, f32[2560]{0:T(1024)}, u32[]{:S(2)}) copy-start(f32[2560]{0:T(1024)} %copy-done.34) | copy-start | bytes 30724
  696.2 28.4 %collective-permute-start.1 = (f32[3,2560]{1,0:T(4,128)S(1)}, f32[3,2560]{1,0:T(4,128)S(1)}, u32[]{:S(2)}, u32[]{:S(2)}) collective-permute-start(f32[3,2560]{1,0:T(4,128)S(1)} %copy.149), channel_id=1, source_target_pairs={{8,0},{16,8},{24,16},{32,24},{40,32},{48,40},{56,48},{64,56},{72,6... | collective-permute-start | bytes 92168 | tf_op jit(solution)/shard_map/ppermute | solution.py:22
  (6 other events, 6.3 us)
Sparse Core Ops, SparseCore 0:
  65.5 235.2 all-gather.6
  303.7 223.8 all-gather.8
  612.3 36.3 reduce-scatter.3
where the time goes:
time: 818 us; the launch traced here: 814 us
  waiting for transfers between devices  294 us (36%)
  blocking collectives  264 us (32%)
  other arithmetic  117 us (14%)
  local copies, waits for them, and re-layouts  83.9 us (10%)
  matrix products  27.5 us (3%)
  between operations  15.8 us (2%)
  starting transfers between devices  9.19 us (1%)
    all_gather x2, waiting for transfers between devices, carried_in(): pieces = jax.tree.map(lambda part: lax.all_gather(part, axis), value)  294 us
    select_n x62, other arithmetic, lap(): jnp.where(position < mine, new, old)  92.3 us
    psum x1, blocking collectives, body(): lax.psum((d_alog_local, d_skip_local), ('ctx', 'fsdp'))  76.8 us
    psum x1, blocking collectives, body(): summed = lax.psum((d_weight, d_bias), 'ctx')  71.7 us
    all_gather x1, blocking collectives, carried_in(): pieces = jax.tree.map(lambda part: lax.all_gather(part, axis), value)  53.2 us
    mul x62, local copies, waits for them, and re-layouts, compose(): later[0][..., None, None] * earlier[1] + later[1]  40.7 us
    unnamed x2, blocking collectives  40.4 us
    rev x2, local copies, waits for them, and re-layouts, carried_in(): pieces = jax.tree.map(lambda part: part[::-1], pieces)  24.4 us
  transfers between devices with their start and end apart: 5, of which 2 were waited for; matrix products, arithmetic and copies ran while one was open for 16% of the time, Pallas kernels for 0%

commit v1 on v0

--- a/solution.py
+++ b/solution.py
@@ -22,25 +22,25 @@
     return lax.ppermute(value, axis, pairs)
 
 
-def carried_in(value, axis, join, neutral, backward):
-    count, mine = (lax.axis_size(axis), lax.axis_index(axis))
-    pieces = jax.tree.map(lambda part: lax.all_gather(part, axis), value)
-    if backward:
-        pieces = jax.tree.map(lambda part: part[::-1], pieces)
-        mine = count - 1 - mine
-    running = jax.tree.map(
-        lambda part, zero: jnp.full_like(part, 0) + jnp.asarray(zero, part.dtype), value, neutral
-    )
-
-    def lap(position, running):
-        longer = join(running, jax.tree.map(lambda part: part[position], pieces))
-        return jax.tree.map(lambda new, old: jnp.where(position < mine, new, old), longer, running)
-
-    return lax.fori_loop(0, count - 1, lap, running)
-
-
 def compose(earlier, later):
     return (earlier[0] * later[0], later[0][..., None, None] * earlier[1] + later[1])
+
+
+def exclusive_scans(fwd, bwd, axis):
+    count = lax.axis_size(axis)
+    width = 1
+    while 2 * width < count:
+        fwd = compose(from_behind(fwd, axis, width), fwd)
+        bwd = compose(from_behind(bwd, axis, -width), bwd)
+        width *= 2
+    fwd_near = from_behind(fwd, axis, 1)
+    bwd_near = from_behind(bwd, axis, -1)
+    if width + 1 < count:
+        fwd = compose(from_behind(fwd, axis, width + 1), fwd_near)
+        bwd = compose(from_behind(bwd, axis, -(width + 1)), bwd_near)
+    else:
+        fwd, bwd = fwd_near, bwd_near
+    return fwd[1], bwd[1]
 
 
 def body(xbc_raw, dt_raw, a_log, skip, conv_weight, conv_bias, grad_y):
@@ -49,12 +49,11 @@
     per_group = HW // GW
     inner_width = HW * P_SIZE
     blocks = tok_rows // SPAN
-    weight_all, bias_all = (
-        lax.all_gather(conv_weight, "fsdp", axis=1, tiled=True),
-        lax.all_gather(conv_bias, "fsdp", axis=0, tiled=True),
-    )
-    weight_f = weight_all.astype(jnp.float32)
-    bias_f = bias_all.astype(jnp.float32)
+    params_all = lax.all_gather(
+        jnp.concatenate([conv_weight, conv_bias[None]], 0), "fsdp", axis=1, tiled=True
+    ).astype(jnp.float32)
+    weight_f = params_all[:KW]
+    bias_f = params_all[KW]
     tail_rows = raw_rows[tok_rows - (KW - 1) :]
     rows_prev = from_behind(tail_rows, "ctx", 1)
     padded = jnp.concatenate([rows_prev, raw_rows], 0).astype(jnp.float32)
@@ -95,12 +94,7 @@
     back_total = zero_state
     for span_idx in reversed(range(blocks)):
         back_total = local_adj[span_idx] + span_decay[span_idx][..., None, None] * back_total
-    state_in = carried_in((dev_decay, fwd_total), "ctx", compose, (unit_decay, zero_state), False)[
-        1
-    ]
-    adjoint_end = carried_in(
-        (dev_decay, back_total), "ctx", compose, (unit_decay, zero_state), True
-    )[1]
+    state_in, adjoint_end = exclusive_scans((dev_decay, fwd_total), (dev_decay, back_total), "ctx")
     cum_t = jnp.transpose(cum_log, (0, 2, 3, 1))
     lower_mask = jnp.tril(jnp.ones((SPAN, SPAN), bool))
     log_gap = cum_t[..., :, None] - cum_t[..., None, :]
@@ -166,12 +160,18 @@
     )
     d_bias = jnp.sum(d_pre, 0)
     grad_scale = 1.0 / math.sqrt(tok_rows * lax.axis_size("ctx") * lax.axis_size("fsdp"))
-    summed = lax.psum((d_weight, d_bias), "ctx")
-    total_weight, total_bias = (
-        lax.psum_scatter(summed[0], "fsdp", scatter_dimension=1, tiled=True),
-        lax.psum_scatter(summed[1], "fsdp", scatter_dimension=0, tiled=True),
-    )
-    head_alog, head_skip = lax.psum((d_alog_local, d_skip_local), ("ctx", "fsdp"))
+    channels = d_bias.shape[0]
+    packed = jnp.concatenate(
+        [d_weight.reshape(-1), d_bias, d_alog_local, d_skip_local]
+    )
+    packed = lax.psum(packed, ("ctx", "fsdp"))
+    own = channels // lax.axis_size("fsdp")
+    col0 = lax.axis_index("fsdp") * own
+    wb = packed[: (KW + 1) * channels].reshape(KW + 1, channels)
+    wb_own = lax.dynamic_slice_in_dim(wb, col0, own, axis=1)
+    total_weight, total_bias = wb_own[:KW], wb_own[KW]
+    heads_part = packed[(KW + 1) * channels :]
+    head_alog, head_skip = heads_part[:HW], heads_part[HW:]
     return (
         d_raw.astype(jnp.bfloat16)[None],
         d_dt_raw[None],

time: 818 us -> 449 us (0.55)
  waiting for transfers between devices: 294 us -> 133 us
  blocking collectives: 264 us -> 129 us
  starting transfers between devices: 9.19 us -> 99.2 us
  other arithmetic: 117 us -> 44.1 us
  local copies, waits for them, and re-layouts: 83.9 us -> 14.5 us
  between operations: 15.8 us -> 1.57 us
    all_gather x2 -> x0, waiting for transfers between devices: 294 us -> none  [carried_in(): pieces = jax.tree.map(lambda part: lax.all_gather(part, axis), value)]
    ppermute x2 -> x24, waiting for transfers between devices: 0.01 us -> 133 us  [from_behind(): return lax.ppermute(value, axis, pairs)]
    select_n x62 -> x1, other arithmetic: 92.3 us -> 0.02 us  [body(): step_size = jax.nn.softplus(steps_raw)]
    ppermute x2 -> x24, starting transfers between devices: 9.07 us -> 99.2 us  [from_behind(): return lax.ppermute(value, axis, pairs)]
    all_gather x2 -> x1, blocking collectives: 75.2 us -> 22.3 us  [body(): lax.all_gather(jnp.concatenate([conv_weight, conv_bias[None]], 0), 'fsdp'...]
    psum x2 -> x1, blocking collectives: 149 us -> 107 us  [body(): packed = lax.psum(packed, ('ctx', 'fsdp'))]
    mul x62 -> x0, local copies, waits for them, and re-layouts: 40.7 us -> none  [compose(): later[0][..., None, None] * earlier[1] + later[1]]
    unnamed x2 -> x0, blocking collectives: 40.4 us -> none
  transfers between devices with their start and end apart: 5 -> 24, of which waited for: 2 -> 7; matrix products, arithmetic and copies ran while one was open for 16% -> 10% of each run, Pallas kernels for 0% -> 0%
where the time goes in v1:
time: 449 us; the launch traced here: 447 us
  waiting for transfers between devices  133 us (30%)
  blocking collectives  129 us (29%)
  starting transfers between devices  99.2 us (22%)
  other arithmetic  44.1 us (10%)
  matrix products  26.2 us (6%)
  local copies, waits for them, and re-layouts  14.5 us (3%)
    ppermute x24, waiting for transfers between devices, from_behind(): return lax.ppermute(value, axis, pairs)  133 us
    psum x1, blocking collectives, body(): packed = lax.psum(packed, ('ctx', 'fsdp'))  107 us
    ppermute x24, starting transfers between devices, from_behind(): return lax.ppermute(value, axis, pairs)  99.2 us
    all_gather x1, blocking collectives, body(): lax.all_gather(jnp.concatenate([conv_weight, conv_bias[None]], 0), 'fsdp'...  22.3 us
    add x7, other arithmetic, compose(): later[0][..., None, None] * earlier[1] + later[1]  10.5 us
  transfers between devices with their start and end apart: 24, of which 7 were waited for; matrix products, arithmetic and copies ran while one was open for 10% of the time, Pallas kernels for 0%

profile of v1, /device:TPU:1, one launch (start us, length us, event | category | flops | bytes accessed | tf_op | source)
XLA Modules:
  0.0 447.0 jit_solution(13302643420018480362)
XLA Ops:
  3.4 5.1 %collective-permute-start.1 = (f32[4,16]{1,0:T(4,128)S(1)}, f32[4,16]{1,0:T(4,128)S(1)}, u32[]{:S(2)}, u32[]{:S(2)}) collective-permute-start(f32[4,16]{1,0:T(4,128)S(1)} %exp.91), channel_id=1, source_target_pairs={{8,0},{16,8},{24,16},{32,24},{40,32},{48,40},{56,48},{64,56},{72,6... | collective-permute-start | bytes 776 | tf_op jit(solution)/shard_map/ppermute | solution.py:22
  8.5 3.0 collective-permute-start.12
  12.4 2.4 collective-permute-start
  15.4 22.3 %all-gather = bf16[8,320,5]{1,2,0:T(8,128)(2,1)S(1)} all-gather(bf16[1,320,5]{1,2,0:T(8,128)(2,1)S(1)} %maximum_bitcast_fusion), channel_id=1, replica_groups=mesh['ctx'=32,'fsdp'=8] {'fsdp'}, dimensions={0}, use_global_device_ids=true | all-gather | bytes 28800 | tf_op jit(solution)/shard_map/all_gather | solution.py:52
  41.2 1.8 maximum_convert_fusion
  43.1 4.0 fusion.25
  49.1 11.6 %collective-permute-start.17 = (f32[4,16,32,64]{3,2,1,0:T(8,128)S(1)}, f32[4,16,32,64]{3,2,1,0:T(8,128)S(1)}, u32[]{:S(2)}, u32[]{:S(2)}) collective-permute-start(f32[4,16,32,64]{3,2,1,0:T(8,128)S(1)} %convolution_add_fusion), channel_id=1, source_target_pairs={{0,8},{8,16},{16,24},{24,32},{32,40},{40,48},{48,56},{56,64},{64,7... | collective-permute-start | bytes 1572872 | tf_op jit(solution)/shard_map/ppermute | solution.py:22
  61.8 1.9 collective-permute-start.6
  63.7 19.9 %collective-permute-done.17 = f32[4,16,32,64]{3,2,1,0:T(8,128)S(1)} collective-permute-done((f32[4,16,32,64]{3,2,1,0:T(8,128)S(1)}, f32[4,16,32,64]{3,2,1,0:T(8,128)S(1)}, u32[]{:S(2)}, u32[]{:S(2)}) %collective-permute-start.17) | collective-permute-done | bytes 524320 | tf_op jit(solution)/shard_map/ppermute | solution.py:22
  83.7 1.6 multiply_add_fusion.4
  85.3 2.3 collective-permute-start.18
  88.9 1.7 copy.138
  90.5 1.3 mul.460
  91.9 1.3 mul.489
  93.8 7.8 %collective-permute-start.13 = (f32[4,16]{1,0:T(4,128)}, f32[4,16]{1,0:T(4,128)}, u32[]{:S(2)}, u32[]{:S(2)}) collective-permute-start(f32[4,16]{1,0:T(4,128)} %get-tuple-element.83), channel_id=1, source_target_pairs={{0,16},{8,24},{16,32},{24,40},{32,48},{40,56},{48,64},{56,72},{64,... | collective-permute-start | bytes 776 | tf_op jit(solution)/shard_map/ppermute | solution.py:22
  102.9 24.3 %collective-permute-done.13 = f32[4,16]{1,0:T(4,128)} collective-permute-done((f32[4,16]{1,0:T(4,128)}, f32[4,16]{1,0:T(4,128)}, u32[]{:S(2)}, u32[]{:S(2)}) %collective-permute-start.13) | collective-permute-done | bytes 288 | tf_op jit(solution)/shard_map/ppermute | solution.py:22
  128.4 6.8 %collective-permute-start.14 = (f32[4,16]{1,0:T(4,128)}, f32[4,16]{1,0:T(4,128)}, u32[]{:S(2)}, u32[]{:S(2)}) collective-permute-start(f32[4,16]{1,0:T(4,128)} %mul.469), channel_id=1, source_target_pairs={{0,32},{8,40},{16,48},{24,56},{32,64},{40,72},{48,80},{56,88},{64,... | collective-permute-start | bytes 776 | tf_op jit(solution)/shard_map/ppermute | solution.py:22
  139.1 8.3 %collective-permute-start.15 = (f32[4,16]{1,0:T(4,128)}, f32[4,16]{1,0:T(4,128)}, u32[]{:S(2)}, u32[]{:S(2)}) collective-permute-start(f32[4,16]{1,0:T(4,128)} %mul.470), channel_id=1, source_target_pairs={{0,64},{8,72},{16,80},{24,88},{32,96},{40,104},{48,112},{56,120},{... | collective-permute-start | bytes 776 | tf_op jit(solution)/shard_map/ppermute | solution.py:22
  150.7 8.0 %collective-permute-start.16 = (f32[4,16]{1,0:T(4,128)S(1)}, f32[4,16]{1,0:T(4,128)}, u32[]{:S(2)}, u32[]{:S(2)}) collective-permute-start(f32[4,16]{1,0:T(4,128)S(1)} %mul.471), channel_id=1, source_target_pairs={{0,8},{8,16},{16,24},{24,32},{32,40},{40,48},{48,56},{56,64},{64,7... | collective-permute-start | bytes 776 | tf_op jit(solution)/shard_map/ppermute | solution.py:22
  159.9 1.7 multiply_add_fusion.3
  161.7 5.5 %collective-permute-start.19 = (f32[4,16,32,64]{3,2,1,0:T(8,128)S(1)}, f32[4,16,32,64]{3,2,1,0:T(8,128)S(1)}, u32[]{:S(2)}, u32[]{:S(2)}) collective-permute-start(f32[4,16,32,64]{3,2,1,0:T(8,128)S(1)} %multiply_add_fusion.3), channel_id=1, source_target_pairs={{0,32},{8,40},{16,48},{24,56},{32,64},{40,72},{48,80},{56,88},{64,... | collective-permute-start | bytes 1572872 | tf_op jit(solution)/shard_map/ppermute | solution.py:22
  167.2 1.7 multiply_add_fusion.10
  168.9 1.3 collective-permute-start.8
  170.8 18.9 %collective-permute-done.19 = f32[4,16,32,64]{3,2,1,0:T(8,128)S(1)} collective-permute-done((f32[4,16,32,64]{3,2,1,0:T(8,128)S(1)}, f32[4,16,32,64]{3,2,1,0:T(8,128)S(1)}, u32[]{:S(2)}, u32[]{:S(2)}) %collective-permute-start.19) | collective-permute-done | bytes 524320 | tf_op jit(solution)/shard_map/ppermute | solution.py:22
  190.6 7.2 %collective-permute-start.20 = (f32[4,16,32,64]{3,2,1,0:T(8,128)S(1)}, f32[4,16,32,64]{3,2,1,0:T(8,128)S(1)}, u32[]{:S(2)}, u32[]{:S(2)}) collective-permute-start(f32[4,16,32,64]{3,2,1,0:T(8,128)S(1)} %multiply_add_fusion.2), channel_id=1, source_target_pairs={{0,64},{8,72},{16,80},{24,88},{32,96},{40,104},{48,112},{56,120},{... | collective-permute-start | bytes 1572872 | tf_op jit(solution)/shard_map/ppermute | solution.py:22
  200.0 6.6 %fusion.4 = (f32[4,16,128]{2,1,0:T(8,128)}, f32[4,16,128]{2,1,0:T(8,128)}, f32[4,128,128]{1,2,0:T(8,128)S(1)}) fusion(f32[4,16,128]{2,1,0:T(8,128)S(1)} %copy-done.24, f32[4,128,128]{1,2,0:T(8,128)S(1)} %fusion.54, pred[128,128]{0,1:T(8,128)(4,1)S(1)} %copy-done.31, bf16[128,4,16,32]{0,3,2,1:T(8,128)(2,1)S(1)} %bitcast.135, ...), kind=kOutput, calls=%fused_computation.10 | convolution fusion | flops 412270592 | bytes 2244608 | tf_op jit(solution)/shard_map/ctgkp,csgkp->cgkts/dot_general | solution.py:104
  206.6 13.1 %collective-permute-done.20 = f32[4,16,32,64]{3,2,1,0:T(8,128)S(1)} collective-permute-done((f32[4,16,32,64]{3,2,1,0:T(8,128)S(1)}, f32[4,16,32,64]{3,2,1,0:T(8,128)S(1)}, u32[]{:S(2)}, u32[]{:S(2)}) %collective-permute-start.20) | collective-permute-done | bytes 524320 | tf_op jit(solution)/shard_map/ppermute | solution.py:22
  219.7 1.8 multiply_add_fusion.1
  221.6 10.7 %collective-permute-start.21 = (f32[4,16,32,64]{3,2,1,0:T(8,128)}, f32[4,16,32,64]{3,2,1,0:T(8,128)}, u32[]{:S(2)}, u32[]{:S(2)}) collective-permute-start(f32[4,16,32,64]{3,2,1,0:T(8,128)} %multiply_add_fusion.1), channel_id=1, source_target_pairs={{0,136},{8,144},{16,152},{24,160},{32,168},{40,176},{48,184},{56,1... | collective-permute-start | bytes 1572872 | tf_op jit(solution)/shard_map/ppermute | solution.py:22
  232.2 1.9 collective-permute-start.22
  234.2 12.7 %collective-permute-done.9 = f32[4,16,32,64]{3,2,1,0:T(8,128)S(1)} collective-permute-done((f32[4,16,32,64]{3,2,1,0:T(8,128)S(1)}, f32[4,16,32,64]{3,2,1,0:T(8,128)S(1)}, u32[]{:S(2)}, u32[]{:S(2)}) %collective-permute-start.9) | collective-permute-done | bytes 524320 | tf_op jit(solution)/shard_map/ppermute | solution.py:22
  246.9 1.9 multiply_add_fusion.8
  250.1 3.0 collective-permute-start.11
  253.1 5.0 %fusion.11 = f32[1,128,4,16,32]{1,4,3,2,0:T(8,128)} fusion(bf16[128,4,16,32]{0,3,2,1:T(8,128)(2,1)S(1)} %bitcast.136, f32[4,16,128]{2,1,0:T(8,128)S(1)} %copy-done.24, f32[4,128,128]{1,2,0:T(8,128)S(1)} %fusion.54, pred[128,128]{0,1:T(8,128)(4,1)S(1)} %copy-done.31), kind=kOutput, calls=%fused_computation.17 | convolution fusion | flops 406847488 | bytes 1884160 | tf_op jit(solution)/shard_map/cgkts,ctgkp->csgkp/dot_general | solution.py:105
  260.4 1.9 collective-permute-start.5
  262.3 1.4 reduce_sum.172
  263.7 1.4 reduce_sum.173
  266.4 41.0 %collective-permute-done.5 = f32[4,16]{1,0:T(4,128)} collective-permute-done((f32[4,16]{1,0:T(4,128)}, f32[4,16]{1,0:T(4,128)}, u32[]{:S(2)}, u32[]{:S(2)}) %collective-permute-start.5) | collective-permute-done | bytes 288 | tf_op jit(solution)/shard_map/ppermute | solution.py:22
  307.4 3.3 multiply_reduce_fusion.4
  310.7 1.9 fusion.27
  312.7 1.9 fusion.28
  314.7 3.1 multiply_reduce_fusion.5
  317.7 4.2 multiply_reduce_fusion.3
  322.1 2.6 fusion.26
  326.8 106.5 %psum.7 = f32[12928]{0:T(1024)S(1)} all-reduce(f32[12928]{0:T(1024)S(1)} %concatenate.21), channel_id=1, replica_groups=mesh['ctx'=32,'fsdp'=8] {'ctx','fsdp'}, use_global_device_ids=true, to_apply=%region_18.19 | all-reduce | flops 12928 | bytes 103424 | tf_op jit(solution)/shard_map/psum | solution.py:167
  434.9 2.8 collective-permute-start.23
  439.1 2.7 collective-permute-done.23
  442.2 3.7 fusion.36
  (168 shorter events, 38.4 us)
Async XLA Ops:
  0.6 37.2 %copy-start.12 = (f32[1,128,64]{1,2,0:T(8,128)S(1)}, f32[1,128,64]{1,2,0:T(8,128)}, u32[]{:S(2)}) copy-start(f32[1,128,64]{1,2,0:T(8,128)} %param.10) | copy-start | bytes 98308
  0.6 37.4 %copy-start.8 = (bf16[1,128,2560]{2,1,0:T(8,128)(2,1)S(1)}, bf16[1,128,2560]{2,1,0:T(8,128)(2,1)}, u32[]{:S(2)}) copy-start(bf16[1,128,2560]{2,1,0:T(8,128)(2,1)} %param.9) | copy-start | bytes 1966084
  0.7 14.8 %copy-start.39 = (bf16[320]{0:T(512)(128)(2,1)S(1)}, bf16[320]{0:T(512)(128)(2,1)}, u32[]{:S(2)}) copy-start(bf16[320]{0:T(512)(128)(2,1)} %param.14) | copy-start | bytes 1924
  0.7 14.7 %copy-start.37 = (bf16[4,320]{1,0:T(4,128)(2,1)S(1)}, bf16[4,320]{1,0:T(4,128)(2,1)}, u32[]{:S(2)}) copy-start(bf16[4,320]{1,0:T(4,128)(2,1)} %param.13) | copy-start | bytes 7684
  2.0 13.4 %copy-start.27 = (f32[4,16]{1,0:T(4,128)}, f32[4,16]{1,0:T(4,128)S(1)}, u32[]{:S(2)}) copy-start(f32[4,16]{1,0:T(4,128)S(1)} %mul.434) | copy-start | bytes 772
  3.0 36.2 %copy-start.10 = (bf16[1,128,2048]{2,1,0:T(8,128)(2,1)S(1)}, bf16[1,128,2048]{2,1,0:T(8,128)(2,1)}, u32[]{:S(2)}) copy-start(bf16[1,128,2048]{2,1,0:T(8,128)(2,1)} %param.15) | copy-start | bytes 1572868
  3.1 34.9 %copy-start.6 = (f32[1,128,4,16]{3,2,1,0:T(4,128)}, f32[1,128,4,16]{3,2,1,0:T(4,128)S(1)}, u32[]{:S(2)}) copy-start(f32[1,128,4,16]{3,2,1,0:T(4,128)S(1)} %fusion.52) | copy-start | bytes 98308
  3.4 36.0 %copy-start.35 = (f32[4,16]{1,0:T(4,128)}, f32[4,16]{1,0:T(4,128)S(1)}, u32[]{:S(2)}) copy-start(f32[4,16]{1,0:T(4,128)S(1)} %exp.91) | copy-start | bytes 772
  3.4 36.0 %collective-permute-start.1 = (f32[4,16]{1,0:T(4,128)S(1)}, f32[4,16]{1,0:T(4,128)S(1)}, u32[]{:S(2)}, u32[]{:S(2)}) collective-permute-start(f32[4,16]{1,0:T(4,128)S(1)} %exp.91), channel_id=1, source_target_pairs={{8,0},{16,8},{24,16},{32,24},{40,32},{48,40},{56,48},{64,56},{72,6... | collective-permute-start | bytes 776 | tf_op jit(solution)/shard_map/ppermute | solution.py:22
  8.5 30.9 %collective-permute-start.12 = (f32[4,16]{1,0:T(4,128)S(1)}, f32[4,16]{1,0:T(4,128)S(1)}, u32[]{:S(2)}, u32[]{:S(2)}) collective-permute-start(f32[4,16]{1,0:T(4,128)S(1)} %exp.91), channel_id=1, source_target_pairs={{0,8},{8,16},{16,24},{24,32},{32,40},{40,48},{48,56},{56,64},{64,7... | collective-permute-start | bytes 776 | tf_op jit(solution)/shard_map/ppermute | solution.py:22
  12.4 27.7 %collective-permute-start = (bf16[3,2560]{1,0:T(4,128)(2,1)S(1)}, bf16[3,2560]{1,0:T(4,128)(2,1)S(1)}, u32[]{:S(2)}, u32[]{:S(2)}) collective-permute-start(bf16[3,2560]{1,0:T(4,128)(2,1)S(1)} %slice_bitcast_fusion), channel_id=1, source_target_pairs={{0,8},{8,16},{16,24},{24,32},{32,40},{40,48},{48,56},{56,64},{64,7... | collective-permute-start | bytes 46088 | tf_op jit(solution)/shard_map/ppermute | solution.py:22
  38.1 5.0 %copy-start.17 = (f32[2560]{0:T(1024)}, f32[2560]{0:T(1024)S(1)}, u32[]{:S(2)}) copy-start(f32[2560]{0:T(1024)S(1)} %get-tuple-element.59) | copy-start | bytes 30724
  38.1 5.0 %copy-start.19 = (f32[2560]{0:T(1024)}, f32[2560]{0:T(1024)S(1)}, u32[]{:S(2)}) copy-start(f32[2560]{0:T(1024)S(1)} %get-tuple-element.60) | copy-start | bytes 30724
  38.1 5.0 %copy-start.21 = (f32[2560]{0:T(1024)}, f32[2560]{0:T(1024)S(1)}, u32[]{:S(2)}) copy-start(f32[2560]{0:T(1024)S(1)} %get-tuple-element.61) | copy-start | bytes 30724
  48.0 13.7 %copy-start = (f32[128,2048]{0,1:T(8,128)}, f32[128,2048]{0,1:T(8,128)S(1)}, u32[]{:S(2)}) copy-start(f32[128,2048]{0,1:T(8,128)S(1)} %get-tuple-element.74) | copy-start | bytes 3145732
  48.0 12.7 %copy-start.13 = (f32[128,4,16]{0,2,1:T(8,128)S(1)}, f32[128,4,16]{0,2,1:T(8,128)}, u32[]{:S(2)}) copy-start(f32[128,4,16]{0,2,1:T(8,128)} %get-tuple-element.82) | copy-start | bytes 98308
  49.1 34.5 %copy-start.36 = (f32[4,16]{1,0:T(4,128)S(1)}, f32[4,16]{1,0:T(4,128)}, u32[]{:S(2)}) copy-start(f32[4,16]{1,0:T(4,128)} %copy-done.35) | copy-start | bytes 772
  49.1 34.5 %collective-permute-start.17 = (f32[4,16,32,64]{3,2,1,0:T(8,128)S(1)}, f32[4,16,32,64]{3,2,1,0:T(8,128)S(1)}, u32[]{:S(2)}, u32[]{:S(2)}) collective-permute-start(f32[4,16,32,64]{3,2,1,0:T(8,128)S(1)} %convolution_add_fusion), channel_id=1, source_target_pairs={{0,8},{8,16},{16,24},{24,32},{32,40},{40,48},{48,56},{56,64},{64,7... | collective-permute-start | bytes 1572872 | tf_op jit(solution)/shard_map/ppermute | solution.py:22
  61.8 21.9 %collective-permute-start.6 = (f32[4,16,32,64]{3,2,1,0:T(8,128)S(1)}, f32[4,16,32,64]{3,2,1,0:T(8,128)S(1)}, u32[]{:S(2)}, u32[]{:S(2)}) collective-permute-start(f32[4,16,32,64]{3,2,1,0:T(8,128)S(1)} %convolution_add_fusion.1), channel_id=1, source_target_pairs={{8,0},{16,8},{24,16},{32,24},{40,32},{48,40},{56,48},{64,56},{72,6... | collective-permute-start | bytes 1572872 | tf_op jit(solution)/shard_map/ppermute | solution.py:22
  85.3 74.7 %collective-permute-start.18 = (f32[4,16,32,64]{3,2,1,0:T(8,128)}, f32[4,16,32,64]{3,2,1,0:T(8,128)}, u32[]{:S(2)}, u32[]{:S(2)}) collective-permute-start(f32[4,16,32,64]{3,2,1,0:T(8,128)} %get-tuple-element.86), channel_id=1, source_target_pairs={{0,16},{8,24},{16,32},{24,40},{32,48},{40,56},{48,64},{56,72},{64,... | collective-permute-start | bytes 1572872 | tf_op jit(solution)/shard_map/ppermute | solution.py:22
  87.6 79.6 %collective-permute-start.7 = (f32[4,16,32,64]{3,2,1,0:T(8,128)}, f32[4,16,32,64]{3,2,1,0:T(8,128)}, u32[]{:S(2)}, u32[]{:S(2)}) collective-permute-start(f32[4,16,32,64]{3,2,1,0:T(8,128)} %get-tuple-element.87), channel_id=1, source_target_pairs={{16,0},{24,8},{32,16},{40,24},{48,32},{56,40},{64,48},{72,56},{80,... | collective-permute-start | bytes 1572872 | tf_op jit(solution)/shard_map/ppermute | solution.py:22
  93.8 33.4 %collective-permute-start.13 = (f32[4,16]{1,0:T(4,128)}, f32[4,16]{1,0:T(4,128)}, u32[]{:S(2)}, u32[]{:S(2)}) collective-permute-start(f32[4,16]{1,0:T(4,128)} %get-tuple-element.83), channel_id=1, source_target_pairs={{0,16},{8,24},{16,32},{24,40},{32,48},{40,56},{48,64},{56,72},{64,... | collective-permute-start | bytes 776 | tf_op jit(solution)/shard_map/ppermute | solution.py:22
  101.6 33.7 %collective-permute-start.2 = (f32[4,16]{1,0:T(4,128)}, f32[4,16]{1,0:T(4,128)}, u32[]{:S(2)}, u32[]{:S(2)}) collective-permute-start(f32[4,16]{1,0:T(4,128)} %get-tuple-element.84), channel_id=1, source_target_pairs={{16,0},{24,8},{32,16},{40,24},{48,32},{56,40},{64,48},{72,56},{80,... | collective-permute-start | bytes 776 | tf_op jit(solution)/shard_map/ppermute | solution.py:22
  128.4 9.4 %collective-permute-start.14 = (f32[4,16]{1,0:T(4,128)}, f32[4,16]{1,0:T(4,128)}, u32[]{:S(2)}, u32[]{:S(2)}) collective-permute-start(f32[4,16]{1,0:T(4,128)} %mul.469), channel_id=1, source_target_pairs={{0,32},{8,40},{16,48},{24,56},{32,64},{40,72},{48,80},{56,88},{64,... | collective-permute-start | bytes 776 | tf_op jit(solution)/shard_map/ppermute | solution.py:22
  136.5 10.9 %collective-permute-start.3 = (f32[4,16]{1,0:T(4,128)}, f32[4,16]{1,0:T(4,128)}, u32[]{:S(2)}, u32[]{:S(2)}) collective-permute-start(f32[4,16]{1,0:T(4,128)} %mul.440), channel_id=1, source_target_pairs={{32,0},{40,8},{48,16},{56,24},{64,32},{72,40},{80,48},{88,56},{96,... | collective-permute-start | bytes 776 | tf_op jit(solution)/shard_map/ppermute | solution.py:22
  139.1 10.9 %collective-permute-start.15 = (f32[4,16]{1,0:T(4,128)}, f32[4,16]{1,0:T(4,128)}, u32[]{:S(2)}, u32[]{:S(2)}) collective-permute-start(f32[4,16]{1,0:T(4,128)} %mul.470), channel_id=1, source_target_pairs={{0,64},{8,72},{16,80},{24,88},{32,96},{40,104},{48,112},{56,120},{... | collective-permute-start | bytes 776 | tf_op jit(solution)/shard_map/ppermute | solution.py:22
  148.7 10.0 %collective-permute-start.4 = (f32[4,16]{1,0:T(4,128)}, f32[4,16]{1,0:T(4,128)}, u32[]{:S(2)}, u32[]{:S(2)}) collective-permute-start(f32[4,16]{1,0:T(4,128)} %mul.441), channel_id=1, source_target_pairs={{64,0},{72,8},{80,16},{88,24},{96,32},{104,40},{112,48},{120,56},{... | collective-permute-start | bytes 776 | tf_op jit(solution)/shard_map/ppermute | solution.py:22
  150.7 109.7 %collective-permute-start.16 = (f32[4,16]{1,0:T(4,128)S(1)}, f32[4,16]{1,0:T(4,128)}, u32[]{:S(2)}, u32[]{:S(2)}) collective-permute-start(f32[4,16]{1,0:T(4,128)S(1)} %mul.471), channel_id=1, source_target_pairs={{0,8},{8,16},{16,24},{24,32},{32,40},{40,48},{48,56},{56,64},{64,7... | collective-permute-start | bytes 776 | tf_op jit(solution)/shard_map/ppermute | solution.py:22
  159.9 7.3 %copy-start.30 = (f32[4,16]{1,0:T(4,128)S(1)}, f32[4,16]{1,0:T(4,128)}, u32[]{:S(2)}) copy-start(f32[4,16]{1,0:T(4,128)} %get-tuple-element.84) | copy-start | bytes 772
  161.7 28.1 %collective-permute-start.19 = (f32[4,16,32,64]{3,2,1,0:T(8,128)S(1)}, f32[4,16,32,64]{3,2,1,0:T(8,128)S(1)}, u32[]{:S(2)}, u32[]{:S(2)}) collective-permute-start(f32[4,16,32,64]{3,2,1,0:T(8,128)S(1)} %multiply_add_fusion.3), channel_id=1, source_target_pairs={{0,32},{8,40},{16,48},{24,56},{32,64},{40,72},{48,80},{56,88},{64,... | collective-permute-start | bytes 1572872 | tf_op jit(solution)/shard_map/ppermute | solution.py:22
  168.9 28.9 %collective-permute-start.8 = (f32[4,16,32,64]{3,2,1,0:T(8,128)S(1)}, f32[4,16,32,64]{3,2,1,0:T(8,128)S(1)}, u32[]{:S(2)}, u32[]{:S(2)}) collective-permute-start(f32[4,16,32,64]{3,2,1,0:T(8,128)S(1)} %multiply_add_fusion.10), channel_id=1, source_target_pairs={{32,0},{40,8},{48,16},{56,24},{64,32},{72,40},{80,48},{88,56},{96,... | collective-permute-start | bytes 1572872 | tf_op jit(solution)/shard_map/ppermute | solution.py:22
  190.6 9.4 %copy-start.1 = (f32[128,2048]{0,1:T(8,128)S(1)}, f32[128,2048]{0,1:T(8,128)}, u32[]{:S(2)}) copy-start(f32[128,2048]{0,1:T(8,128)} %copy-done) | copy-start | bytes 3145732
  190.6 9.4 %copy-start.24 = (f32[4,16,128]{2,1,0:T(8,128)S(1)}, f32[4,16,128]{2,1,0:T(8,128)}, u32[]{:S(2)}) copy-start(f32[4,16,128]{2,1,0:T(8,128)} %copy.138) | copy-start | bytes 98308
  190.6 9.4 %copy-start.31 = (pred[128,128]{0,1:T(8,128)(4,1)S(1)}, pred[128,128]{0,1:T(8,128)(4,1)}, u32[]{:S(2)}) copy-start(pred[128,128]{0,1:T(8,128)(4,1)} %iota_compare_fusion) | copy-start | bytes 49156
  190.6 29.1 %collective-permute-start.20 = (f32[4,16,32,64]{3,2,1,0:T(8,128)S(1)}, f32[4,16,32,64]{3,2,1,0:T(8,128)S(1)}, u32[]{:S(2)}, u32[]{:S(2)}) collective-permute-start(f32[4,16,32,64]{3,2,1,0:T(8,128)S(1)} %multiply_add_fusion.2), channel_id=1, source_target_pairs={{0,64},{8,72},{16,80},{24,88},{32,96},{40,104},{48,112},{56,120},{... | collective-permute-start | bytes 1572872 | tf_op jit(solution)/shard_map/ppermute | solution.py:22
  198.7 48.2 %collective-permute-start.9 = (f32[4,16,32,64]{3,2,1,0:T(8,128)S(1)}, f32[4,16,32,64]{3,2,1,0:T(8,128)S(1)}, u32[]{:S(2)}, u32[]{:S(2)}) collective-permute-start(f32[4,16,32,64]{3,2,1,0:T(8,128)S(1)} %multiply_add_fusion.9), channel_id=1, source_target_pairs={{64,0},{72,8},{80,16},{88,24},{96,32},{104,40},{112,48},{120,56},{... | collective-permute-start | bytes 1572872 | tf_op jit(solution)/shard_map/ppermute | solution.py:22
  221.6 85.8 %collective-permute-start.21 = (f32[4,16,32,64]{3,2,1,0:T(8,128)}, f32[4,16,32,64]{3,2,1,0:T(8,128)}, u32[]{:S(2)}, u32[]{:S(2)}) collective-permute-start(f32[4,16,32,64]{3,2,1,0:T(8,128)} %multiply_add_fusion.1), channel_id=1, source_target_pairs={{0,136},{8,144},{16,152},{24,160},{32,168},{40,176},{48,184},{56,1... | collective-permute-start | bytes 1572872 | tf_op jit(solution)/shard_map/ppermute | solution.py:22
  232.2 75.1 %collective-permute-start.22 = (f32[4,16,32,64]{3,2,1,0:T(8,128)}, f32[4,16,32,64]{3,2,1,0:T(8,128)}, u32[]{:S(2)}, u32[]{:S(2)}) collective-permute-start(f32[4,16,32,64]{3,2,1,0:T(8,128)} %multiply_add_fusion.1), channel_id=1, source_target_pairs={{0,8},{8,16},{16,24},{24,32},{32,40},{40,48},{48,56},{56,64},{64,7... | collective-permute-start | bytes 1572872 | tf_op jit(solution)/shard_map/ppermute | solution.py:22
  248.8 58.6 %collective-permute-start.10 = (f32[4,16,32,64]{3,2,1,0:T(8,128)}, f32[4,16,32,64]{3,2,1,0:T(8,128)}, u32[]{:S(2)}, u32[]{:S(2)}) collective-permute-start(f32[4,16,32,64]{3,2,1,0:T(8,128)} %multiply_add_fusion.8), channel_id=1, source_target_pairs={{136,0},{144,8},{152,16},{160,24},{168,32},{176,40},{184,48},{192,... | collective-permute-start | bytes 1572872 | tf_op jit(solution)/shard_map/ppermute | solution.py:22
  250.1 57.3 %collective-permute-start.11 = (f32[4,16,32,64]{3,2,1,0:T(8,128)}, f32[4,16,32,64]{3,2,1,0:T(8,128)}, u32[]{:S(2)}, u32[]{:S(2)}) collective-permute-start(f32[4,16,32,64]{3,2,1,0:T(8,128)} %multiply_add_fusion.8), channel_id=1, source_target_pairs={{8,0},{16,8},{24,16},{32,24},{40,32},{48,40},{56,48},{64,56},{72,6... | collective-permute-start | bytes 1572872 | tf_op jit(solution)/shard_map/ppermute | solution.py:22
  260.4 47.0 %collective-permute-start.5 = (f32[4,16]{1,0:T(4,128)}, f32[4,16]{1,0:T(4,128)}, u32[]{:S(2)}, u32[]{:S(2)}) collective-permute-start(f32[4,16]{1,0:T(4,128)} %mul.442), channel_id=1, source_target_pairs={{8,0},{16,8},{24,16},{32,24},{40,32},{48,40},{56,48},{64,56},{72,6... | collective-permute-start | bytes 776 | tf_op jit(solution)/shard_map/ppermute | solution.py:22
  266.4 44.4 %copy-start.2 = (f32[128,2048]{0,1:T(8,128)S(1)}, f32[128,2048]{0,1:T(8,128)}, u32[]{:S(2)}) copy-start(f32[128,2048]{0,1:T(8,128)} %copy-done) | copy-start | bytes 3145732
  266.4 44.4 %copy-start.11 = (f32[4,64,128]{2,1,0:T(8,128)S(1)}, f32[4,64,128]{2,1,0:T(8,128)}, u32[]{:S(2)}) copy-start(f32[4,64,128]{2,1,0:T(8,128)} %fusion.55) | copy-start | bytes 393220
  324.8 109.8 %copy-start.3 = (f32[128,2560]{0,1:T(8,128)S(1)}, f32[128,2560]{0,1:T(8,128)}, u32[]{:S(2)}) copy-start(f32[128,2560]{0,1:T(8,128)} %get-tuple-element.63) | copy-start | bytes 3932164
  434.5 7.7 %copy-start.18 = (f32[2560]{0:T(1024)S(1)}, f32[2560]{0:T(1024)}, u32[]{:S(2)}) copy-start(f32[2560]{0:T(1024)} %copy-done.17) | copy-start | bytes 30724
  434.5 7.7 %copy-start.20 = (f32[2560]{0:T(1024)S(1)}, f32[2560]{0:T(1024)}, u32[]{:S(2)}) copy-start(f32[2560]{0:T(1024)} %copy-done.19) | copy-start | bytes 30724
  434.5 7.7 %copy-start.22 = (f32[2560]{0:T(1024)S(1)}, f32[2560]{0:T(1024)}, u32[]{:S(2)}) copy-start(f32[2560]{0:T(1024)} %copy-done.21) | copy-start | bytes 30724
  434.9 6.8 %collective-permute-start.23 = (f32[3,2560]{1,0:T(4,128)S(1)}, f32[3,2560]{1,0:T(4,128)S(1)}, u32[]{:S(2)}, u32[]{:S(2)}) collective-permute-start(f32[3,2560]{1,0:T(4,128)S(1)} %copy.147), channel_id=1, source_target_pairs={{8,0},{16,8},{24,16},{32,24},{40,32},{48,40},{56,48},{64,56},{72,6... | collective-permute-start | bytes 92168 | tf_op jit(solution)/shard_map/ppermute | solution.py:22
  (16 other events, 36.9 us)
